TPU v7x, 32 devices: a whole 2x2x4 slice. The times are simulated.
32 devices in a mesh: img: 4 (over y, x), freq: 8 (over z, core).
Axes of the slice: x: 2, y: 2, z: 4, core: 2. Of those that a mesh axis runs over, the one named last changes fastest.
Arguments:
- images: bfloat16 [2, 6144, 32768], P(None, 'img', 'freq'), may hold values from -6 to 6
- references: bfloat16 [2, 896, 32768], P(None, 'img', 'freq'), may hold values from -6 to 6
- noise_weight: float32 [32768], P('freq'), may hold values from 0.005 to 0.05
- prior_orient: int32 [6144], P('img'), may hold values from 0 to 895
- segment_brick: int32 [8, 896, 32, 1], P('freq', 'img'), may hold values from 0 to 31; in each aligned block of 7168 rows (0 to 7167, 7168 to 14335, ..., all dimensions but the last counted through in order) at most 560 rows name the same one
- segment_row: int32 [8, 896, 32], P('freq', 'img'), may hold values from 0 to 1999
- segment_kernel: int32 [8, 896, 32], P('freq', 'img'), may hold values from 0 to 7
- kernel_taps: float32 [8, 4], replicated, may hold values from 0.1 to 1
Outputs:
- posterior: float32 [896, 6144], P('freq', 'img')
- volume: float32 [32, 2, 2000, 128], P(('img', 'freq'))
Inputs may be any that keep to these rules, and one draw needn't show every extreme that they name: `segment_brick`: counted in aligned blocks of 7168 segments in the map's order, no brick is named more than 560 times within one block, a bound that some block reaches.
All inputs are finite; a program needn't handle non-finite values.
Results may differ from a plain program's by a relative error of at most 0.014.
Values may be sent and summed in bfloat16 or wider, within the bound.
No kernel may reach another device: no remote copies, remote signals or barrier semaphores. Data moves between devices by JAX's collectives and lax.ppermute only.
A program may use at most 128 MiB of HBM per device.

v0:
```python
import jax
import jax.numpy as jnp
from jax import lax
from jax.sharding import PartitionSpec as P

BROWS = 2000


tempering = 0.5
masked_logit = -1e30
contract_last = (((1,), (1,)), ((), ()))


def spread_taps(values, kernels, kernel_taps):
    phases = kernel_taps.shape[0]
    tap_count = kernel_taps.shape[1]
    member = (kernels[:, None] == jnp.arange(phases, dtype=jnp.int32)[None, :]).astype(
        kernel_taps.dtype
    )
    factors = jnp.dot(member, kernel_taps, precision=lax.Precision.HIGHEST)
    padded = jnp.pad(values, ((0, 0), (0, 0), (tap_count - 2, 1)))
    lane_count = values.shape[2]
    result = jnp.zeros(values.shape, values.dtype)
    for tap_index in range(tap_count):
        first_lane = tap_count - 1 - tap_index
        result = (
            result
            + factors[:, tap_index, None, None] * padded[:, :, first_lane : first_lane + lane_count]
        )
    return result


def window_logits(scores, orient_index, prior_orient, orient_count):
    distance = (orient_index[:, None] - prior_orient[None, :]) % orient_count
    half_window = orient_count // 8
    allowed = (distance <= half_window) | (distance >= orient_count - half_window)
    return jnp.where(allowed, tempering * scores, masked_logit)


def on_device(
    images,
    references,
    noise_weight,
    prior_orient,
    segment_brick,
    segment_row,
    segment_kernel,
    kernel_taps,
):
    image_groups = lax.axis_size("img")
    freq_groups = lax.axis_size("freq")
    local_orients = references.shape[1]
    orient_count = local_orients * image_groups
    share_rows = orient_count // freq_groups
    unpacked = lax.all_gather(references, "img", axis=1, tiled=True).astype(jnp.float32)
    weighted = (noise_weight * unpacked).astype(jnp.bfloat16)
    energies = jnp.sum(
        noise_weight * (unpacked[0] * unpacked[0] + unpacked[1] * unpacked[1]), axis=1
    )
    products = lax.dot_general(
        weighted[0], images[0], contract_last, preferred_element_type=jnp.float32
    )
    products = products + lax.dot_general(
        weighted[1], images[1], contract_last, preferred_element_type=jnp.float32
    )
    partial_scores = products - 0.5 * energies[:, None]
    scores = lax.psum(partial_scores, "freq")
    logits = window_logits(
        scores, jnp.arange(orient_count, dtype=jnp.int32), prior_orient, orient_count
    )
    highest = jnp.max(logits, axis=0)
    raised = jnp.exp(logits - highest[None, :])
    posterior = raised / jnp.sum(raised, axis=0)[None, :]
    rounded = posterior.astype(jnp.bfloat16)
    own_rows = lax.dynamic_slice_in_dim(
        posterior, lax.axis_index("freq") * share_rows, share_rows, 0
    )
    weighted_sums = lax.psum_scatter(
        jnp.einsum("oi,cif->ocf", rounded, images, preferred_element_type=jnp.float32).astype(
            jnp.bfloat16
        ),
        "img",
        scatter_dimension=0,
        tiled=True,
    ).astype(jnp.float32)
    segment_blocks = segment_row.shape[2]
    lane_count = images.shape[2] // segment_blocks
    local_segments = local_orients * segment_blocks
    values = weighted_sums.reshape(local_orients, 2, segment_blocks, lane_count).transpose(
        0, 2, 1, 3
    )
    values = values.reshape(local_segments, 2, lane_count)
    targets = segment_brick.reshape(local_segments)
    voxel_rows = segment_row.reshape(local_segments)
    kernels = segment_kernel.reshape(local_segments)
    brick_count = image_groups * freq_groups
    capacity = max(2, 5 * local_segments // (2 * brick_count))
    segment_ids = jnp.arange(local_segments, dtype=jnp.int32)
    same_brick = (targets[:, None] == targets[None, :]) & (
        segment_ids[None, :] < segment_ids[:, None]
    )
    rank_within = jnp.sum(same_brick.astype(jnp.int32), axis=1)
    places = targets * capacity + rank_within
    slot_total = brick_count * capacity
    slot_ids = jnp.arange(slot_total, dtype=jnp.int32)
    slot_hits = places[None, :] == slot_ids[:, None]
    occupied = jnp.any(slot_hits, axis=1)
    source_index = jnp.max(jnp.where(slot_hits, segment_ids[None, :], 0), axis=1)

    def pack_slots(source):
        picked = jnp.take(source, source_index, axis=0)
        mask_shape = (slot_total,) + (1,) * (source.ndim - 1)
        packed = jnp.where(occupied.reshape(mask_shape), picked, jnp.zeros((), source.dtype))
        return packed.reshape((brick_count, capacity) + source.shape[1:])

    arrived, arrived_rows = (
        lax.all_to_all(
            pack_slots(spread_taps(values, kernels, kernel_taps)).astype(jnp.bfloat16),
            ("img", "freq"),
            split_axis=0,
            concat_axis=1,
            tiled=True,
        ).astype(jnp.float32),
        lax.all_to_all(
            pack_slots(voxel_rows), ("img", "freq"), split_axis=0, concat_axis=1, tiled=True
        ),
    )
    contributions = arrived.reshape(-1, 2, lane_count)
    row_count = BROWS
    row_member = (
        arrived_rows.reshape(-1)[None, :] == jnp.arange(row_count, dtype=jnp.int32)[:, None]
    )
    flat_terms = contributions.reshape(-1, 2 * lane_count)
    volume = jnp.dot(row_member.astype(jnp.float32), flat_terms, precision=lax.Precision.HIGHEST)
    volume = volume.reshape(row_count, 2, lane_count)
    return (own_rows, volume.transpose(1, 0, 2)[None])


def solution(mesh):
    in_specs = (
        P(None, "img", "freq"),
        P(None, "img", "freq"),
        P("freq"),
        P("img"),
        P("freq", "img", None, None),
        P("freq", "img", None),
        P("freq", "img", None),
        P(),
    )
    out_specs = (P("freq", "img"), P(("img", "freq"), None, None, None))
    return jax.shard_map(
        on_device, mesh=mesh, in_specs=in_specs, out_specs=out_specs, check_vma=False
    )
```

profile of v0, /device:TPU:0, one launch (start us, length us, event | category | flops | bytes accessed | tf_op | source)
XLA Modules:
  0.0 1126.2 jit_solution(3930945149105243404)
XLA Ops:
  7.2 0.7 all-gather.2.cloned.1.call-update
  8.0 144.5 %all-gather.2.cloned.1.call-done = bf16[2,896,4096]{2,1,0:T(8,128)(2,1)} async-done(((bf16[2,224,4096]{2,1,0:T(8,128)(2,1)}), bf16[2,896,4096]{2,1,0:T(8,128)(2,1)}) %all-gather.2.cloned.1.call-update) | async-done | bytes 14680080 | tf_op jit(solution)/shard_map/all_gather | solution.py:55
  152.4 8.6 convert_element_type.24
  161.0 2.7 fusion.9
  163.7 8.5 multiply_convert_fusion
  172.2 15.9 %fusion.10 = f32[896,1536]{1,0:T(8,128)} fusion(bf16[2,1536,4096]{2,1,0:T(8,128)(2,1)} %param.8, bf16[2,896,4096]{2,1,0:T(8,128)(2,1)S(1)} %multiply_convert_fusion), kind=kOutput, calls=%fused_computation.23 | convolution fusion | flops 11274289152 | bytes 25427968 | tf_op jit(solution)/shard_map/dot_general | solution.py:63
  188.1 16.5 %add_subtract_fusion = f32[896,1536]{1,0:T(8,128)} fusion(f32[896,1536]{1,0:T(8,128)} %fusion.10, bf16[2,1536,4096]{2,1,0:T(8,128)(2,1)} %param.8, bf16[2,896,4096]{2,1,0:T(8,128)(2,1)S(1)} %multiply_convert_fusion, f32[896]{0:T(1024)S(1)} %broadcast_multiply_fusion), kind=kOutput, calls=%fused_computation.42 | convolution fusion | flops 11277041664 | bytes 30937088 | tf_op jit(solution)/shard_map/dot_general | solution.py:60
  205.1 120.8 %all-reduce.3.cloned.1.call-done = f32[896,1536]{1,0:T(8,128)} async-done(((f32[896,1536]{1,0:T(8,128)}), f32[896,1536]{1,0:T(8,128)}) %all-reduce.3.cloned.1.call-update) | async-done | bytes 5505040 | tf_op jit(solution)/shard_map/psum | solution.py:67
  326.0 6.1 fusion.40
  332.1 0.8 fusion.29
  332.9 0.7 fusion.28
  333.6 2.4 copy-done.1
  336.0 28.2 %convolution_convert_fusion = bf16[896,2,4096]{2,0,1:T(8,128)(2,1)} fusion(bf16[2,1536,4096]{2,1,0:T(8,128)(2,1)} %param.8, f32[896,1536]{1,0:T(8,128)S(1)} %fusion.28), kind=kOutput, calls=%fused_computation.29 | convolution fusion | flops 22557294592 | bytes 45350912 | tf_op jit(solution)/shard_map/oi,cif->ocf/dot_general | solution.py:79
  364.3 0.7 copy-done.3
  365.4 54.7 %convert_reduce_fusion = s32[7168]{0:T(1024)S(1)} fusion(s32[7168]{0:T(1024)S(1)} %reshape.147), kind=kLoop, calls=%fused_computation.5 | loop fusion | flops 256893952 | bytes 57344 | tf_op jit(solution)/shard_map/reduce_sum | solution.py:102
  420.1 88.3 %select_reduce_fusion = s32[17920]{0:T(1024)S(1)} fusion(s32[7168]{0:T(1024)S(1)} %multiply_add_fusion), kind=kLoop, calls=%fused_computation.2 | loop fusion | flops 385333760 | bytes 100352 | tf_op jit(solution)/shard_map/reduce_max | solution.py:108
  508.8 92.1 %gather_fusion = s32[17920]{0:T(1024)S(1)} fusion(s32[7168]{0:T(1024)S(1)} %reshape.148, s32[18432]{0:T(1024)S(1)} %pad_clamp_fusion), kind=kCustom, calls=%fused_computation | custom fusion | bytes 215040 | tf_op jit(solution)/shard_map/jit(_take)/gather | solution.py:111
  601.0 77.3 %fusion = pred[17920]{0:T(1024)(128)(4,1)S(1)} fusion(s32[7168]{0:T(1024)S(1)} %multiply_add_fusion), kind=kLoop, calls=%fused_computation.4 | loop fusion | flops 256883200 | bytes 46592 | tf_op jit(solution)/shard_map/reduce_or | solution.py:107
  678.4 0.7 copy.24
  679.2 4.8 all-to-all-start
  684.9 2.9 reshape.155
  687.8 4.6 copy.28
  692.4 13.4 %copy.26 = f32[224,32,2,128]{3,2,1,0:T(2,128)} copy(f32[224,32,2,128]{3,1,0,2:T(8,128)} %bitcast.66) | data formatting | bytes 14680064 | tf_op jit(solution)/shard_map/reshape | solution.py:92
  705.7 62.7 %fusion.19 = bf16[7168,2,128]{2,1,0:T(2,128)(2,1)} fusion(f32[7168,2,128]{2,1,0:T(2,128)} %bitcast.67, f32[7168]{0:T(1024)S(1)} %bitcast.71, f32[7168]{0:T(1024)S(1)} %bitcast.72, f32[7168]{0:T(1024)S(1)} %bitcast.73, f32[7168]{0:T(1024)S(1)} %bitcast.70), kind=kLoop, calls=%fused_computation.35 | loop fusion | flops 14680064 | bytes 11124736 | tf_op jit(solution)/shard_map/add | solution.py:27
  768.4 45.9 %gather_fusion.1 = bf16[17920,2,128]{2,1,0:T(2,128)(2,1)} fusion(bf16[7168,2,128]{2,1,0:T(2,128)(2,1)} %fusion.19, s32[18432]{0:T(1024)S(1)} %pad_clamp_fusion), kind=kCustom, calls=%fused_computation.1 | custom fusion | bytes 18421760 | tf_op jit(solution)/shard_map/jit(_take)/gather | solution.py:111
  814.3 45.3 %select_convert_fusion = bf16[32,560,2,128]{3,2,1,0:T(2,128)(2,1)} fusion(bf16[32,560,2,128]{3,2,1,0:T(2,128)(2,1)} %bitcast.64, pred[32,560]{1,0:T(8,128)(4,1)S(1)} %compare_and_fusion, pred[32,560]{1,0:T(8,128)(4,1)S(1)} %broadcast_in_dim.69), kind=kLoop, calls=%fused_computation.13 | loop fusion | flops 9175040 | bytes 18385920 | tf_op jit(solution)/shard_map/convert_element_type | solution.py:118
  859.6 6.1 all-to-all-start.1
  866.0 2.0 constant_dynamic-slice_fusion
  868.0 199.3 %all-to-all-done.1 = bf16[32,560,2,128]{3,2,1,0:T(2,128)(2,1)} async-done(((bf16[32,560,2,128]{3,2,1,0:T(2,128)(2,1)}), bf16[32,560,2,128]{3,2,1,0:T(2,128)(2,1)}, u32[]{:S(2)}, u32[]{:S(2)}) %all-to-all-start.1) | async-done | bytes 9175072 | tf_op jit(solution)/shard_map/all_to_all | solution.py:117
  1067.3 9.3 copy.31
  1076.7 12.6 %copy.27 = bf16[256,17920]{1,0:T(8,128)(2,1)} copy(bf16[256,17920]{0,1:T(8,128)(2,1)} %bitcast.65) | data formatting | bytes 18350080 | tf_op jit(solution)/shard_map/dot_general | solution.py:134
  1089.2 30.2 %fusion.34 = f32[1,2,2000,128]{3,2,1,0:T(8,128)} fusion(bf16[2,128,17920]{2,1,0:T(8,128)(2,1)} %bitcast.69, s32[17920]{0:T(1024)S(1)} %eq.64), kind=kOutput, calls=%fused_computation.54 | convolution fusion | flops 18385920000 | bytes 11294720 | tf_op jit(solution)/shard_map/dot_general | solution.py:134
  (40 shorter events, 2.7 us)
Async XLA Ops:
  7.2 677.3 %copy-start = (f32[8,4]{0,1:T(4,128)S(1)}, f32[8,4]{0,1:T(4,128)}, u32[]{:S(2)}) copy-start(f32[8,4]{0,1:T(4,128)} %param.15) | copy-start | bytes 388
  7.2 145.3 %all-gather.2.cloned.1.call-start = ((), (), s32[]{:S(2)}) async-start(), calls=%async_computation.3 | async-start | bytes 18350080 | tf_op jit(solution)/shard_map/all_gather | solution.py:55
  7.9 153.1 %copy-start.2 = (f32[4096]{0:T(1024)S(1)}, f32[4096]{0:T(1024)}, u32[]{:S(2)}) copy-start(f32[4096]{0:T(1024)} %param.10) | copy-start | bytes 49156
  7.9 318.0 %all-reduce.3.cloned.1.call-start = ((), (), s32[]{:S(2)}) async-start(), calls=%async_computation.4 | async-start | bytes 11010048 | tf_op jit(solution)/shard_map/psum | solution.py:67
  188.1 137.9 %copy-start.6 = (s32[1536]{0:T(1024)S(1)}, s32[1536]{0:T(1024)}, u32[]{:S(2)}) copy-start(s32[1536]{0:T(1024)} %param.11) | copy-start | bytes 18436
  204.6 480.2 %reduce-scatter.2.cloned.1.call-start = ((), (), s32[]{:S(2)}) async-start(), calls=%async_computation.5 | async-start | bytes 18350080 | tf_op jit(solution)/shard_map/reduce_scatter | solution.py:78
  333.6 2.4 copy-start.1
  364.3 0.8 copy-start.3
  364.3 1.0 copy-start.4
  508.7 175.5 %copy-start.5 = (s32[1,224,32]{1,2,0:T(8,128)S(1)}, s32[1,224,32]{1,2,0:T(8,128)}, u32[]{:S(2)}) copy-start(s32[1,224,32]{1,2,0:T(8,128)} %param.14) | copy-start | bytes 86020
  679.2 180.5 %all-to-all-start = ((s32[32,1,560]{2,1,0:T(1,128)}), s32[32,1,560]{2,1,0:T(1,128)S(1)}, u32[]{:S(2)}, u32[]{:S(2)}) async-start(s32[32,1,560]{2,1,0:T(1,128)} %copy.24), calls=%async_computation | async-start | bytes 163840 | tf_op jit(solution)/shard_map/all_to_all | solution.py:124
  859.6 207.7 %all-to-all-start.1 = ((bf16[32,560,2,128]{3,2,1,0:T(2,128)(2,1)}), bf16[32,560,2,128]{3,2,1,0:T(2,128)(2,1)}, u32[]{:S(2)}, u32[]{:S(2)}) async-start(bf16[32,560,2,128]{3,2,1,0:T(2,128)(2,1)} %select_convert_fusion), calls=%async_computation.2 | async-start | bytes 18350080 | tf_op jit(solution)/shard_map/all_to_all | solution.py:117
Sparse Core Ops, SparseCore 0:
  9.8 142.5 all-gather.1
  204.7 121.1 all-reduce.2
  364.4 137.7 reduce-scatter.1
where the time goes:
time: 1130 us
  waiting for transfers between devices  465 us (41%)
  other arithmetic  359 us (32%)
  local copies, waits for them, and re-layouts  185 us (16%)
  matrix products  91.1 us (8%)
  between operations  14.3 us (1%)
  starting transfers between devices  11.5 us (1%)
    all_to_all x1, waiting for transfers between devices, on_device(): lax.all_to_all(pack_slots(spread_taps(values, kernels, kernel_taps)).asty...  199 us
    all_gather x1, waiting for transfers between devices, on_device(): lax.all_gather(references, 'img', axis=1, tiled=True).astype(jnp.float32)  144 us
    gather x3, local copies, waits for them, and re-layouts, pack_slots(): picked = jnp.take(source, source_index, axis=0)  138 us
    psum x1, waiting for transfers between devices, on_device(): scores = lax.psum(partial_scores, 'freq')  121 us
    reduce_max x1, other arithmetic, on_device(): jnp.max(jnp.where(slot_hits, segment_ids[None, :], 0), axis=1)  88.3 us
    reduce_or x1, other arithmetic, on_device(): occupied = jnp.any(slot_hits, axis=1)  77.3 us
    add x1, other arithmetic, spread_taps(): result + factors[:, tap_index, None, None] * padded[:, :, first_lane:firs...  62.7 us
    reduce_sum x1, other arithmetic, on_device(): rank_within = jnp.sum(same_brick.astype(jnp.int32), axis=1)  54.7 us
  transfers between devices with their start and end apart: 5, of which 3 were waited for; matrix products, arithmetic and copies ran while one was open for 44% of the time, Pallas kernels for 0%

commit v1 on v0

v1 whole, which is shorter than its diff:
```python
import functools

import jax
import jax.numpy as jnp
from jax import lax
from jax.experimental import pallas as pl
from jax.experimental.pallas import tpu as pltpu
from jax.sharding import PartitionSpec as P

BROWS = 2000
LANES = 128

tempering = 0.5
contract_last = (((1,), (1,)), ((), ()))
VMEM_BYTES = 60 * 1024 * 1024


def round_up(value, multiple):
    return -(-value // multiple) * multiple


def window_start(prior, half_window, orient_count):
    start = prior - half_window
    return jnp.where(start < 0, start + orient_count, start)


def bits_of(count):
    bit = 1
    while bit < count:
        yield bit
        bit *= 2


def cut_windows(half_window, prior_ref, score_ref, out_ref):
    orient_count = score_ref.shape[0]
    keep = out_ref.shape[0]
    for lanes in range(0, out_ref.shape[1], LANES):
        cols = slice(lanes, lanes + LANES)
        start = window_start(prior_ref[:, cols], half_window, orient_count)
        x = score_ref[:, cols]
        for bit in reversed(list(bits_of(orient_count))):
            kept = min(orient_count, round_up(bit - 1 + keep, 8))
            if bit >= 8:
                moved = jnp.concatenate([x[bit:], x[:bit]], axis=0)
            else:
                moved = pltpu.roll(x, x.shape[0] - bit, axis=0)
            x = jnp.where((start & bit) != 0, moved[:kept], x[:kept])
        out_ref[:, cols] = x


def cut_kernel(half_window, prior_ref, score_ref, out_ref):
    cut_windows(half_window, prior_ref, score_ref, out_ref)


def tail_kernel(half_window, own_ref, prior_ref, b0_ref, b1_ref, b2_ref, b3_ref, image_ref,
                w_first_ref, w_second_ref, out_ref, score_ref):
    block = b0_ref.shape[0]
    part = w_first_ref.shape[0]
    own = own_ref[0]

    def rows_of(relative):
        return pl.multiple_of((own ^ relative) * block, 8)

    for relative, ref in enumerate((b0_ref, b1_ref, b2_ref)):
        score_ref[pl.ds(rows_of(relative), block), :] = ref[...]
    image = image_ref[...]
    for index, ref in enumerate((w_first_ref, w_second_ref)):
        here = pl.ds(pl.multiple_of(rows_of(3) + index * part, 8), part)
        score_ref[here, :] = b3_ref[index * part : (index + 1) * part, :] + lax.dot_general(
            ref[...], image, contract_last, preferred_element_type=jnp.float32
        )
    cut_windows(half_window, prior_ref, score_ref, out_ref)


def spread_kernel(half_window, order, own_ref, prior_ref, score_ref, full_ref, share_ref, wide_ref):
    orient_count = wide_ref.shape[0]
    width = 2 * half_window + 1
    own, share = own_ref[0], own_ref[1]
    for lanes in range(0, score_ref.shape[1], LANES):
        cols = slice(lanes, lanes + LANES)
        start = window_start(prior_ref[:, cols], half_window, orient_count)
        scores = score_ref[:, cols]
        place = lax.broadcasted_iota(jnp.int32, scores.shape, 0)
        logits = jnp.where(place < width, tempering * scores, -1e30)
        highest = jnp.max(logits, axis=0, keepdims=True)
        raised = jnp.exp(logits - highest)
        x = raised / jnp.sum(raised, axis=0, keepdims=True)
        for bit in bits_of(orient_count):
            grown = min(orient_count, round_up(x.shape[0] + bit, 8))
            extra = grown - x.shape[0]
            if extra:
                x = jnp.concatenate([x, jnp.zeros((extra, LANES), x.dtype)], axis=0)
            if bit >= 8:
                moved = jnp.concatenate([x[-bit:], x[:-bit]], axis=0)
            else:
                moved = pltpu.roll(x, bit, axis=0)
            x = jnp.where((start & bit) != 0, moved, x)
        wide_ref[:, cols] = x
    if order is None:
        full_ref[...] = wide_ref[...].astype(full_ref.dtype)
    else:
        block = orient_count // len(order)
        for index, relative in enumerate(order):
            here = pl.ds(pl.multiple_of((own ^ relative) * block, 8), block)
            full_ref[index * block : (index + 1) * block, :] = wide_ref[here, :].astype(
                full_ref.dtype
            )
    share_rows = share_ref.shape[0]
    share_ref[...] = wide_ref[pl.ds(pl.multiple_of(share * share_rows, 8), share_rows), :]


def slot_rows_kernel(slot_ref, row_ref, out_ref):
    slot_total = out_ref.shape[0]
    count = slot_ref.shape[0]

    def clear(step, carry):
        for part in range(16):
            out_ref[step * 16 + part] = -1
        return carry

    lax.fori_loop(0, slot_total // 16, clear, 0)

    def fill(step, carry):
        places = [slot_ref[step * 16 + part] for part in range(16)]
        taken = [row_ref[step * 16 + part] for part in range(16)]
        for slot, row in zip(places, taken):
            out_ref[slot] = row
        return carry

    lax.fori_loop(0, count // 16, fill, 0)


def pack_kernel(slot_ref, *refs):
    factor_ref, out_ref, value_ref, taken_ref, slots_ref = refs[-5:]
    pieces = (len(refs) - 5) // 2
    step = pl.program_id(0)
    rows, lane_count = value_ref.shape

    def add_up(*refs):
        total = refs[0][...].astype(jnp.float32)
        for ref in refs[1:]:
            total = total + ref[...].astype(jnp.float32)
        value_ref[...] = total

    first = step < pl.num_programs(0) // 2
    pl.when(first)(lambda: add_up(*refs[:pieces]))
    pl.when(jnp.logical_not(first))(lambda: add_up(*refs[pieces : 2 * pieces]))
    chunk = 128
    slot_total = slots_ref.shape[0]

    @pl.when(step == 0)
    def _():
        def clear(index, carry):
            slots_ref[pl.ds(pl.multiple_of(index * chunk, chunk), chunk), :] = jnp.zeros(
                (chunk, lane_count), jnp.float32
            )
            return carry

        lax.fori_loop(0, slot_total // chunk, clear, 0)

    values = value_ref[...]
    lane = lax.broadcasted_iota(jnp.int32, values.shape, 1)
    factors = factor_ref[...]
    total = jnp.zeros(values.shape, jnp.float32)
    for tap in range(factors.shape[1]):
        offset = 1 - tap
        moved = values
        if offset:
            moved = pltpu.roll(values, (-offset) % lane_count, axis=1)
            source = lane + offset
            moved = jnp.where((source >= 0) & (source < lane_count), moved, 0.0)
        total = total + factors[:, tap : tap + 1] * moved
    taken_ref[...] = total
    base = step * rows

    def place(index, carry):
        first_row = index * 16
        places = [slot_ref[base + first_row + part] for part in range(16)]
        taken = [taken_ref[pl.ds(first_row + part, 1), :] for part in range(16)]
        for slot, row in zip(places, taken):
            slots_ref[pl.ds(slot, 1), :] = row
        return carry

    lax.fori_loop(0, rows // 16, place, 0)

    @pl.when(step == pl.num_programs(0) - 1)
    def _():
        def narrow(index, carry):
            here = pl.ds(pl.multiple_of(index * chunk, chunk), chunk)
            out_ref[here, :] = slots_ref[here, :].astype(out_ref.dtype)
            return carry

        lax.fori_loop(0, slot_total // chunk, narrow, 0)


def add_rounded(left, right):
    return (left.astype(jnp.float32) + right.astype(jnp.float32)).astype(jnp.bfloat16)


def params(**kwargs):
    return pltpu.CompilerParams(vmem_limit_bytes=VMEM_BYTES, **kwargs)


def window(
    images,
    references,
    noise_weight,
    prior_orient,
    segment_brick,
    segment_row,
    segment_kernel,
    kernel_taps,
):
    image_groups = lax.axis_size("img")
    freq_groups = lax.axis_size("freq")
    local_orients, local_freqs = references.shape[1:]
    image_count = images.shape[1]
    orient_count = local_orients * image_groups
    share_rows = orient_count // freq_groups
    half_window = orient_count // 8
    width = 2 * half_window + 1
    keep = round_up(width, 8)
    brick_count = image_groups * freq_groups

    by_neighbours = image_groups == 4
    order = (0, 1, 3, 2) if by_neighbours else None

    def across(value, offset):
        pairs = [(source, source ^ offset) for source in range(image_groups)]
        return lax.ppermute(value, "img", pairs)

    unpacked = references.astype(jnp.float32)
    half_rows = local_orients // 2
    blocks = []
    for part in range(2):
        own = (noise_weight * unpacked[part]).astype(jnp.bfloat16)
        if not by_neighbours:
            blocks.append(lax.all_gather(own, "img", axis=0, tiled=True))
            continue
        beside = across(own, 1)
        above = across(own, 2)
        blocks.append(
            (
                own,
                beside,
                above,
                across(beside[:half_rows], 2),
                across(above[half_rows:], 1),
            )
        )
    energies = jnp.sum(
        noise_weight * (unpacked[0] * unpacked[0] + unpacked[1] * unpacked[1]), axis=1
    )
    if by_neighbours:
        energies = [energies] + [across(energies, offset) for offset in (1, 2, 3)]
    else:
        energies = lax.all_gather(energies, "img", axis=0, tiled=True)

    segment_blocks = segment_row.shape[2]
    lane_count = local_freqs // segment_blocks
    local_segments = local_orients * segment_blocks
    targets = segment_brick.reshape(local_orients, segment_blocks).T.reshape(local_segments)
    voxel_rows = segment_row.reshape(local_orients, segment_blocks).T.reshape(local_segments)
    kernels = segment_kernel.reshape(local_orients, segment_blocks).T
    capacity = round_up(max(2, 5 * local_segments // (2 * brick_count)), 16)
    slot_total = brick_count * capacity
    named = (targets[:, None] == jnp.arange(brick_count, dtype=jnp.int32)[None, :]).astype(
        jnp.bfloat16
    )
    run = 128
    runs = local_segments // run
    lower = jnp.tril(jnp.ones((run, run), jnp.bfloat16))
    within = jnp.einsum(
        "ab,nbk->nak",
        lower,
        named.reshape(runs, run, brick_count),
        preferred_element_type=jnp.float32,
    )
    ahead = jnp.dot(
        jnp.tril(jnp.ones((runs, runs), jnp.bfloat16), -1),
        within[:, -1, :].astype(jnp.bfloat16),
        preferred_element_type=jnp.float32,
    )
    ranks = jnp.sum(
        named.reshape(runs, run, brick_count).astype(jnp.float32) * (within + ahead[:, None, :]),
        axis=2,
    ).reshape(local_segments)
    slots = targets * capacity + ranks.astype(jnp.int32) - 1
    slot_rows = pl.pallas_call(
        slot_rows_kernel,
        out_shape=jax.ShapeDtypeStruct((slot_total,), jnp.int32),
        in_specs=[pl.BlockSpec(memory_space=pltpu.SMEM)] * 2,
        out_specs=pl.BlockSpec(memory_space=pltpu.SMEM),
    )(slots, voxel_rows)
    arrived_rows = lax.all_to_all(
        slot_rows.reshape(brick_count, capacity), ("img", "freq"), 0, 0, tiled=True
    )
    phases = jnp.arange(kernel_taps.shape[0], dtype=jnp.int32)
    factors = jnp.dot(
        (kernels[..., None] == phases).astype(jnp.float32),
        kernel_taps,
        precision=lax.Precision.HIGHEST,
    )

    def scores_of(weights, part):
        return lax.dot_general(
            weights, images[part], contract_last, preferred_element_type=jnp.float32
        )

    cols = 256
    image_steps = (image_count // cols,)
    prior_row = prior_orient.reshape(1, image_count)
    prior_spec = pl.BlockSpec((1, cols), lambda i: (0, i))
    scalar_spec = pl.BlockSpec(memory_space=pltpu.SMEM)
    whole_spec = pl.BlockSpec((half_rows, local_freqs), lambda i: (0, 0))
    block_spec = pl.BlockSpec((local_orients, cols), lambda i: (0, i))
    keep_spec = pl.BlockSpec((keep, cols), lambda i: (0, i))
    place = jnp.stack([lax.axis_index("img"), lax.axis_index("freq")]).astype(jnp.int32)
    if by_neighbours:
        before = [
            lax.optimization_barrier(scores_of(blocks[0][index], 0))
            + (scores_of(blocks[1][index], 1) - 0.5 * energies[index][:, None])
            for index in range(3)
        ]
        opposite = jnp.concatenate(blocks[0][3:], axis=0)
        before.append(scores_of(opposite, 0) - 0.5 * energies[3][:, None])
        partial_scores = pl.pallas_call(
            functools.partial(tail_kernel, half_window),
            grid=image_steps,
            out_shape=jax.ShapeDtypeStruct((keep, image_count), jnp.float32),
            in_specs=[scalar_spec, prior_spec]
            + [block_spec] * 4
            + [pl.BlockSpec((None, cols, local_freqs), lambda i: (1, i, 0))]
            + [whole_spec] * 2,
            out_specs=keep_spec,
            scratch_shapes=[pltpu.VMEM((orient_count, cols), jnp.float32)],
            compiler_params=params(),
        )(place, prior_row, *before, images, blocks[1][3], blocks[1][4])
    else:
        complete = scores_of(blocks[0], 0) + scores_of(blocks[1], 1) - 0.5 * energies[:, None]
        partial_scores = pl.pallas_call(
            functools.partial(cut_kernel, half_window),
            grid=image_steps,
            out_shape=jax.ShapeDtypeStruct((keep, image_count), jnp.float32),
            in_specs=[prior_spec, pl.BlockSpec((orient_count, cols), lambda i: (0, i))],
            out_specs=keep_spec,
            compiler_params=params(),
        )(prior_row, complete)
    scores = lax.psum(partial_scores, "freq")
    rounded, own_rows = pl.pallas_call(
        functools.partial(spread_kernel, half_window, order),
        grid=image_steps,
        out_shape=(
            jax.ShapeDtypeStruct((orient_count, image_count), jnp.bfloat16),
            jax.ShapeDtypeStruct((share_rows, image_count), jnp.float32),
        ),
        in_specs=[scalar_spec, prior_spec, keep_spec],
        out_specs=(
            pl.BlockSpec((orient_count, cols), lambda i: (0, i)),
            pl.BlockSpec((share_rows, cols), lambda i: (0, i)),
        ),
        scratch_shapes=[pltpu.VMEM((orient_count, cols), jnp.float32)],
        compiler_params=params(),
    )(place, prior_row, scores)

    row_member = (
        arrived_rows.reshape(-1)[None, :] == jnp.arange(BROWS, dtype=jnp.int32)[:, None]
    ).astype(jnp.bfloat16)
    half_freqs = local_freqs // 2
    one, two, three = local_orients, 2 * local_orients, 3 * local_orients

    left, right = slice(0, half_freqs), slice(half_freqs, local_freqs)

    def sums(weights, part, rows, cols):
        return jnp.dot(
            weights[rows], images[part, :, cols], preferred_element_type=jnp.float32
        ).astype(jnp.bfloat16)

    def first_sends(weights, part):
        return (
            sums(weights, part, slice(one, three), left),
            sums(weights, part, slice(two, None), right),
        )

    def second_sends(weights, part, sends):
        beside = across(sends[0], 1)
        above = across(sends[1], 2)
        kept = sums(weights, part, slice(0, two), right)
        passed = (
            add_rounded(sums(weights, part, slice(three, None), left), beside[one:]),
            add_rounded(kept[one:], above[:one]),
        )
        return beside, above, kept, passed

    if by_neighbours:
        sends = first_sends(rounded, 0)
        beside, above, kept, passed = second_sends(rounded, 0, sends)
        last = across(passed[0], 2), across(passed[1], 1)
        pieces = [[sums(rounded, 0, slice(0, one), left), beside, last[0], kept, above, last[1]]]
        later = lax.optimization_barrier((rounded, *passed))[0]
        sends = first_sends(later, 1)
        pieces[0][0] = lax.optimization_barrier((pieces[0][0], *sends))[0]
        beside, above, kept, passed = second_sends(later, 1, sends)
        last = across(passed[0], 2), across(passed[1], 1)
        pieces.append([sums(later, 1, slice(0, one), left), beside, last[0], kept, above, last[1]])
    else:
        pieces = []
        for part in range(2):
            summed = lax.psum_scatter(
                sums(rounded, part, slice(None), slice(None)),
                "img",
                scatter_dimension=0,
                tiled=True,
            )
            pieces.append([summed[:, left], summed[:, right]])

    half_steps = segment_blocks // 2

    def first_half(row):
        return pl.BlockSpec((one, lane_count), lambda j: (row, jnp.minimum(j, half_steps - 1)))

    def second_half(row):
        return pl.BlockSpec((one, lane_count), lambda j: (row, jnp.maximum(j - half_steps, 0)))

    if by_neighbours:
        value_specs = [first_half(0)] * 3 + [second_half(0), second_half(1), second_half(0)]
    else:
        value_specs = [first_half(0), second_half(0)]
    volumes = []
    for part in range(2):
        pack = pl.pallas_call(
            pack_kernel,
            grid=(segment_blocks,),
            out_shape=jax.ShapeDtypeStruct((slot_total, lane_count), jnp.bfloat16),
            in_specs=[
                pl.BlockSpec(memory_space=pltpu.SMEM),
                *value_specs,
                pl.BlockSpec((None,) + factors.shape[1:], lambda j: (j, 0, 0)),
            ],
            out_specs=pl.BlockSpec((slot_total, lane_count), lambda j: (0, 0)),
            scratch_shapes=[
                pltpu.VMEM((local_orients, lane_count), jnp.float32),
                pltpu.VMEM((local_orients, lane_count), jnp.float32),
                pltpu.VMEM((slot_total, lane_count), jnp.float32),
            ],
            compiler_params=params(),
        )
        packed = pack(slots, *pieces[part], factors)
        arrived = lax.all_to_all(
            packed.reshape(brick_count, capacity, lane_count),
            ("img", "freq"),
            0,
            0,
            tiled=True,
        ).reshape(slot_total, lane_count)
        volumes.append(jnp.dot(row_member, arrived, preferred_element_type=jnp.float32))
    return own_rows, jnp.stack(volumes)[None]


def solution(mesh):
    in_specs = (
        P(None, "img", "freq"),
        P(None, "img", "freq"),
        P("freq"),
        P("img"),
        P("freq", "img", None, None),
        P("freq", "img", None),
        P("freq", "img", None),
        P(),
    )
    out_specs = (P("freq", "img"), P(("img", "freq"), None, None, None))
    return jax.shard_map(window, mesh=mesh, in_specs=in_specs, out_specs=out_specs, check_vma=False)
```

time: 1130 us -> 639 us (0.57)
  other arithmetic: 359 us -> 12.7 us
  waiting for transfers between devices: 465 us -> 266 us
  local copies, waits for them, and re-layouts: 185 us -> 9.79 us
  Pallas kernels: 0 us -> 122 us
  matrix products: 91.1 us -> 164 us
  starting transfers between devices: 11.5 us -> 40.2 us
    ppermute x0 -> x19, waiting for transfers between devices: none -> 178 us  [across(): return lax.ppermute(value, 'img', pairs)]
    all_gather x1 -> x0, waiting for transfers between devices: 144 us -> none  [on_device(): lax.all_gather(references, 'img', axis=1, tiled=True).astype(jnp.float32)]
    gather x3 -> x0, local copies, waits for them, and re-layouts: 138 us -> none  [pack_slots(): picked = jnp.take(source, source_index, axis=0)]
    pallas_call x0 -> x5, Pallas kernels: none -> 122 us  [the longest x2 61 us: window(): packed = pack(slots, *pieces[part], factors)]
    all_to_all x2 -> x3, waiting for transfers between devices: 199 us -> 79.1 us  [the longest x2 79.1 us: window(): lax.all_to_all(packed.reshape(brick_count, capacity, lane_count), ('img',...]
    psum x1, waiting for transfers between devices: 121 us -> 9.5 us  [window(): scores = lax.psum(partial_scores, 'freq')]
    reduce_max x2 -> x0, other arithmetic: 94.4 us -> none  [the longest x1 88.3 us: on_device(): jnp.max(jnp.where(slot_hits, segment_ids[None, :], 0), axis=1)]
    reduce_or x1 -> x0, other arithmetic: 77.3 us -> none  [on_device(): occupied = jnp.any(slot_hits, axis=1)]
  transfers between devices with their start and end apart: 5 -> 23, of which waited for: 3 -> 13; matrix products, arithmetic and copies ran while one was open for 44% -> 24% of each run, Pallas kernels for 0% -> 17%
where the time goes in v1:
time: 639 us; the launch traced here: 629 us
  waiting for transfers between devices  266 us (42%)
  matrix products  164 us (26%)
  Pallas kernels  122 us (19%)
  starting transfers between devices  40.2 us (6%)
  between operations  14.7 us (2%)
  other arithmetic  12.7 us (2%)
  local copies, waits for them, and re-layouts  9.79 us (2%)
    ppermute x19, waiting for transfers between devices, across(): return lax.ppermute(value, 'img', pairs)  178 us
    all_to_all x2, waiting for transfers between devices, window(): lax.all_to_all(packed.reshape(brick_count, capacity, lane_count), ('img',...  79.1 us
    pallas_call x2, Pallas kernels, window(): packed = pack(slots, *pieces[part], factors)  61 us
    dot_general x7, matrix products, scores_of(): lax.dot_general(weights, images[part], contract_last, preferred_element_t...  60.3 us
    dot_general x10, matrix products, sums(): jnp.dot(weights[rows], images[part, :, cols], preferred_element_type=jnp....  51.4 us
    dot_general x2, matrix products, window(): jnp.dot(row_member, arrived, preferred_element_type=jnp.float32)  47.8 us
    pallas_call x1, Pallas kernels, window(): pl.pallas_call(slot_rows_kernel, out_shape=jax.ShapeDtypeStruct((slot_tot...  39.9 us
    ppermute x19, starting transfers between devices, across(): return lax.ppermute(value, 'img', pairs)  25.6 us
  transfers between devices with their start and end apart: 23, of which 13 were waited for; matrix products, arithmetic and copies ran while one was open for 24% of the time, Pallas kernels for 17%

profile of v1, /device:TPU:0, one launch (start us, length us, event | category | flops | bytes accessed | tf_op | source)
XLA Modules:
  0.0 629.2 jit_solution(1762876248699884687)
XLA Ops:
  21.4 9.6 %fusion.16 = f32[224,1536]{1,0:T(8,128)} fusion(bf16[2,1536,4096]{2,1,0:T(8,128)(2,1)} %image_ref.1, f32[2,224,4096]{2,1,0:T(8,128)S(1)} %convert_element_type.104, f32[4096]{0:T(1024)S(1)} %copy-done.14), kind=kOutput, calls=%fused_computation.17 | convolution fusion | flops 2820407296 | bytes 17645568 | tf_op jit(solution)/shard_map/dot_general | solution.py:306
  31.6 11.0 %fusion.84.b0_ref = f32[224,1536]{1,0:T(8,128)} fusion(f32[224,1536]{1,0:T(8,128)} %fusion.16, bf16[2,1536,4096]{2,1,0:T(8,128)(2,1)} %image_ref.1, f32[2,224,4096]{2,1,0:T(8,128)} %copy-done.2, f32[4096]{0:T(1024)S(1)} %copy-done.14, f32[224]{0:T(256)S(1)} %broadcast_multiply_fusion.4), kind=kOutput, calls=%fused_computation.75 | convolution fusion | flops 2821095424 | bytes 19022720 | tf_op jit(solution)/shard_map/dot_general | solution.py:306
  44.6 13.3 %collective-permute-done.8 = f32[224]{0:T(256)S(1)} collective-permute-done((f32[224]{0:T(256)S(1)}, f32[224]{0:T(256)S(1)}, u32[]{:S(2)}, u32[]{:S(2)}) %collective-permute-start.8) | collective-permute-done | bytes 928 | tf_op jit(solution)/shard_map/ppermute | solution.py:230
  64.6 7.6 %fusion.12 = f32[224,1536]{1,0:T(8,128)S(1)} fusion(bf16[224,4096]{1,0:T(8,128)(2,1)} %collective-permute-done.3, bf16[2,1536,4096]{2,1,0:T(8,128)(2,1)} %image_ref.1), kind=kOutput, calls=%fused_computation.13 | convolution fusion | flops 2818572288 | bytes 15794176 | tf_op jit(solution)/shard_map/dot_general | solution.py:306
  72.2 7.5 %fusion.14 = f32[224,1536]{1,0:T(8,128)S(1)} fusion(bf16[224,4096]{1,0:T(8,128)(2,1)} %collective-permute-done, bf16[2,1536,4096]{2,1,0:T(8,128)(2,1)} %image_ref.1), kind=kOutput, calls=%fused_computation.15 | convolution fusion | flops 2818572288 | bytes 15794176 | tf_op jit(solution)/shard_map/dot_general | solution.py:306
  79.7 21.0 %collective-permute-done.4 = bf16[224,4096]{1,0:T(8,128)(2,1)S(1)} collective-permute-done((bf16[224,4096]{1,0:T(8,128)(2,1)S(1)}, bf16[224,4096]{1,0:T(8,128)(2,1)S(1)}, u32[]{:S(2)}, u32[]{:S(2)}) %collective-permute-start.4) | collective-permute-done | bytes 1835040 | tf_op jit(solution)/shard_map/ppermute | solution.py:230
  104.2 6.9 %fusion.90 = f32[224,1536]{1,0:T(8,128)S(1)} fusion(bf16[224,4096]{1,0:T(8,128)(2,1)S(1)} %collective-permute-done.4, bf16[2,1536,4096]{2,1,0:T(8,128)(2,1)} %image_ref.1, f32[224]{0:T(256)S(1)} %broadcast_multiply_fusion.2), kind=kOutput, calls=%fused_computation.77 | convolution fusion | flops 2818916352 | bytes 15795072 | tf_op jit(solution)/shard_map/dot_general | solution.py:306
  112.4 7.5 %fusion.87 = f32[224,1536]{1,0:T(8,128)S(1)} fusion(bf16[224,4096]{1,0:T(8,128)(2,1)} %collective-permute-done.1, bf16[2,1536,4096]{2,1,0:T(8,128)(2,1)} %image_ref.1, f32[224]{0:T(256)S(1)} %broadcast_multiply_fusion.3), kind=kOutput, calls=%fused_computation.76 | convolution fusion | flops 2818916352 | bytes 15795072 | tf_op jit(solution)/shard_map/dot_general | solution.py:306
  121.1 10.1 %fusion.78.b3_ref = f32[224,1536]{1,0:T(8,128)} fusion(bf16[2,1536,4096]{2,1,0:T(8,128)(2,1)} %image_ref.1, bf16[112,4096]{1,0:T(8,128)(2,1)} %collective-permute-done.7, bf16[112,4096]{1,0:T(8,128)(2,1)} %collective-permute-done.6, f32[224]{0:T(256)S(1)} %broadcast_multiply_fusion.1), kind=kOutput, calls=%fused_computation.73 | convolution fusion | flops 2822586368 | bytes 15795072 | tf_op jit(solution)/shard_map/dot_general | solution.py:306
  131.2 6.9 %collective-permute-done.10.w_second_ref = bf16[112,4096]{1,0:T(8,128)(2,1)S(1)} collective-permute-done((bf16[112,4096]{1,0:T(8,128)(2,1)S(1)}, bf16[112,4096]{1,0:T(8,128)(2,1)S(1)}, u32[]{:S(2)}, u32[]{:S(2)}) %collective-permute-start.10) | collective-permute-done | bytes 917536 | tf_op jit(solution)/shard_map/ppermute | solution.py:230
  140.1 14.6 %shard_map.95 = f32[232,1536]{1,0:T(8,128)} custom-call(s32[2]{0:T(128)} %pad_add_fusion.own_ref, s32[1,1536]{1,0:T(1,128)} %reshape.88.prior_ref, f32[224,1536]{1,0:T(8,128)} %fusion.84.b0_ref, f32[224,1536]{1,0:T(8,128)} %add.49.b1_ref, f32[224,1536]{1,0:T(8,128)} %add.50.b2_ref, f32[224,1536]{1,0:T(8,128)} %fusion.78.b3_ref, ...), custom_call_target="tpu_custom_call" | custom-call | tf_op jit(solution)/shard_map/pallas_call | solution.py:327
  156.7 39.9 %shard_map.97 = s32[17920]{0:T(1024)} custom-call(s32[7168]{0:T(1024)} %fusion.151.slot_ref, s32[7168]{0:T(1024)} %reshape.91.row_ref), custom_call_target="tpu_custom_call" | custom-call | tf_op jit(solution)/shard_map/pallas_call | solution.py:289
  198.3 5.7 all-to-all-start
  207.9 9.5 %all-reduce.2.cloned.1.call-done.score_ref = f32[232,1536]{1,0:T(8,128)} async-done(((f32[232,1536]{1,0:T(8,128)}), f32[232,1536]{1,0:T(8,128)}) %all-reduce.2.cloned.1.call-update) | async-done | bytes 1425424 | tf_op jit(solution)/shard_map/psum | solution.py:349
  217.4 6.0 shard_map.96
  223.5 7.6 %fusion.66 = bf16[448,2048]{1,0:T(8,128)(2,1)} fusion(bf16[2,1536,4096]{2,1,0:T(8,128)(2,1)} %image_ref.1, bf16[896,1536]{1,0:T(8,128)(2,1)} %get-tuple-element.8), kind=kOutput, calls=%fused_computation.69 | convolution fusion | flops 2819489792 | bytes 9502720 | tf_op jit(solution)/shard_map/dot_general | solution.py:375
  232.8 7.6 %fusion.60 = bf16[448,2048]{1,0:T(8,128)(2,1)} fusion(bf16[2,1536,4096]{2,1,0:T(8,128)(2,1)} %image_ref.1, bf16[896,1536]{1,0:T(8,128)(2,1)S(1)} %copy-done.16), kind=kOutput, calls=%fused_computation.67 | convolution fusion | flops 2819489792 | bytes 9502720 | tf_op jit(solution)/shard_map/dot_general | solution.py:375
  241.8 5.3 fusion.93.refs_0_
  250.2 22.0 %collective-permute-done.12.refs_4_ = bf16[448,2048]{1,0:T(8,128)(2,1)S(1)} collective-permute-done((bf16[448,2048]{1,0:T(8,128)(2,1)}, bf16[448,2048]{1,0:T(8,128)(2,1)S(1)}, u32[]{:S(2)}, u32[]{:S(2)}) %collective-permute-start.12) | collective-permute-done | bytes 1835040 | tf_op jit(solution)/shard_map/ppermute | solution.py:230
  274.0 9.4 %collective-permute-done.11.refs_1_ = bf16[448,2048]{1,0:T(8,128)(2,1)S(1)} collective-permute-done((bf16[448,2048]{1,0:T(8,128)(2,1)}, bf16[448,2048]{1,0:T(8,128)(2,1)S(1)}, u32[]{:S(2)}, u32[]{:S(2)}) %collective-permute-start.11) | collective-permute-done | bytes 1835040 | tf_op jit(solution)/shard_map/ppermute | solution.py:230
  294.9 5.7 collective-permute-done.14.refs_5_
  303.3 30.5 %shard_map.98 = bf16[17920,128]{1,0:T(8,128)(2,1)} custom-call(s32[7168]{0:T(1024)} %fusion.151.slot_ref, bf16[224,2048]{1,0:T(8,128)(2,1)} %fusion.93.refs_0_, bf16[448,2048]{1,0:T(8,128)(2,1)} %copy-done.8, bf16[224,2048]{1,0:T(8,128)(2,1)} %collective-permute-done.13.refs_2_, bf16[448,2048]{1,0:T(8,128)(2,1)} %copy-done.6, bf16[448,2048]{1,0:T(8,128)(2,1)} %copy-done.3, ...), custom_call_target="tpu_custom_call" | custom-call | tf_op jit(solution)/shard_map/pallas_call | solution.py:448
  340.6 6.2 fusion.75.refs_3_
  346.8 77.1 %collective-permute-done.17.refs_4_ = bf16[448,2048]{1,0:T(8,128)(2,1)S(1)} collective-permute-done((bf16[448,2048]{1,0:T(8,128)(2,1)}, bf16[448,2048]{1,0:T(8,128)(2,1)S(1)}, u32[]{:S(2)}, u32[]{:S(2)}) %collective-permute-start.17) | collective-permute-done | bytes 1835040 | tf_op jit(solution)/shard_map/ppermute | solution.py:230
  432.9 5.3 fusion.102.refs_0_
  438.2 14.4 %collective-permute-done.18.refs_5_ = bf16[224,2048]{1,0:T(8,128)(2,1)} collective-permute-done((bf16[224,2048]{1,0:T(8,128)(2,1)S(1)}, bf16[224,2048]{1,0:T(8,128)(2,1)}, u32[]{:S(2)}, u32[]{:S(2)}) %collective-permute-start.18) | collective-permute-done | bytes 917536 | tf_op jit(solution)/shard_map/ppermute | solution.py:230
  452.6 5.1 collective-permute-done.16.refs_2_
  457.7 30.6 %shard_map.99 = bf16[17920,128]{1,0:T(8,128)(2,1)} custom-call(s32[7168]{0:T(1024)} %fusion.151.slot_ref, bf16[224,2048]{1,0:T(8,128)(2,1)} %fusion.102.refs_0_, bf16[448,2048]{1,0:T(8,128)(2,1)} %copy-done.7, bf16[224,2048]{1,0:T(8,128)(2,1)} %collective-permute-done.16.refs_2_, bf16[448,2048]{1,0:T(8,128)(2,1)} %copy-done.5, bf16[448,2048]{1,0:T(8,128)(2,1)} %copy-done.4, ...), custom_call_target="tpu_custom_call" | custom-call | tf_op jit(solution)/shard_map/pallas_call | solution.py:448
  488.2 5.2 all-to-all-start.2
  493.8 23.9 %fusion.111 = f32[1,2000,128]{2,1,0:T(8,128)S(1)} fusion(bf16[17920,128]{1,0:T(8,128)(2,1)} %bitcast.24, s32[17920]{0:T(1024)S(1)} %eq.49), kind=kOutput, calls=%fused_computation.84 | convolution fusion | flops 9210880000 | bytes 5683200 | tf_op jit(solution)/shard_map/dot_general | solution.py:456
  517.7 79.1 %all-to-all-done.2 = bf16[32,560,128]{2,1,0:T(8,128)(2,1)} async-done(((bf16[32,560,128]{2,1,0:T(8,128)(2,1)}), bf16[32,560,128]{2,1,0:T(8,128)(2,1)}, u32[]{:S(2)}, u32[]{:S(2)}) %all-to-all-start.2) | async-done | bytes 4587552 | tf_op jit(solution)/shard_map/all_to_all | solution.py:449
  596.8 23.9 %fusion.112 = f32[1,2000,128]{2,1,0:T(8,128)S(1)} fusion(bf16[17920,128]{1,0:T(8,128)(2,1)} %bitcast.27, s32[17920]{0:T(1024)S(1)} %eq.49), kind=kOutput, calls=%fused_computation.85 | convolution fusion | flops 9210880000 | bytes 5683200 | tf_op jit(solution)/shard_map/dot_general | solution.py:456
  (122 shorter events, 78.4 us)
Async XLA Ops:
  7.2 196.9 %copy-start = (f32[8,4]{0,1:T(4,128)S(1)}, f32[8,4]{0,1:T(4,128)}, u32[]{:S(2)}) copy-start(f32[8,4]{0,1:T(4,128)} %param.15) | copy-start | bytes 388
  7.2 210.2 %all-reduce.2.cloned.1.call-start = ((), (), s32[]{:S(2)}) async-start(), calls=%async_computation.3 | async-start | bytes 2850816 | tf_op jit(solution)/shard_map/psum | solution.py:349
  13.4 46.5 %collective-permute-start = (bf16[224,4096]{1,0:T(8,128)(2,1)}, bf16[224,4096]{1,0:T(8,128)(2,1)}, u32[]{:S(2)}, u32[]{:S(2)}) collective-permute-start(bf16[224,4096]{1,0:T(8,128)(2,1)} %get-tuple-element.11), channel_id=1, source_target_pairs={{0,8},{8,0},{16,24},{24,16},{1,9},{9,1},{17,25},{25,17},{2,10},{10... | collective-permute-start | bytes 5505032 | tf_op jit(solution)/shard_map/ppermute | solution.py:230
  16.4 46.3 %collective-permute-start.3 = (bf16[224,4096]{1,0:T(8,128)(2,1)}, bf16[224,4096]{1,0:T(8,128)(2,1)}, u32[]{:S(2)}, u32[]{:S(2)}) collective-permute-start(bf16[224,4096]{1,0:T(8,128)(2,1)} %get-tuple-element.11), channel_id=1, source_target_pairs={{0,16},{8,24},{16,0},{24,8},{1,17},{9,25},{17,1},{25,9},{2,18},{10... | collective-permute-start | bytes 5505032 | tf_op jit(solution)/shard_map/ppermute | solution.py:230
  17.9 39.9 %collective-permute-start.8 = (f32[224]{0:T(256)S(1)}, f32[224]{0:T(256)S(1)}, u32[]{:S(2)}, u32[]{:S(2)}) collective-permute-start(f32[224]{0:T(256)S(1)} %get-tuple-element.12), channel_id=1, source_target_pairs={{0,24},{8,16},{16,8},{24,0},{1,25},{9,17},{17,9},{25,1},{2,26},{10... | collective-permute-start | bytes 2696 | tf_op jit(solution)/shard_map/ppermute | solution.py:230
  17.9 40.3 %collective-permute-start.5 = (f32[224]{0:T(256)S(1)}, f32[224]{0:T(256)S(1)}, u32[]{:S(2)}, u32[]{:S(2)}) collective-permute-start(f32[224]{0:T(256)S(1)} %get-tuple-element.12), channel_id=1, source_target_pairs={{0,16},{8,24},{16,0},{24,8},{1,17},{9,25},{17,1},{25,9},{2,18},{10... | collective-permute-start | bytes 2696 | tf_op jit(solution)/shard_map/ppermute | solution.py:230
  19.9 40.0 %collective-permute-start.2 = (f32[224]{0:T(256)S(1)}, f32[224]{0:T(256)S(1)}, u32[]{:S(2)}, u32[]{:S(2)}) collective-permute-start(f32[224]{0:T(256)S(1)} %get-tuple-element.12), channel_id=1, source_target_pairs={{0,8},{8,0},{16,24},{24,16},{1,9},{9,1},{17,25},{25,17},{2,10},{10... | collective-permute-start | bytes 2696 | tf_op jit(solution)/shard_map/ppermute | solution.py:230
  57.9 42.9 %collective-permute-start.4 = (bf16[224,4096]{1,0:T(8,128)(2,1)S(1)}, bf16[224,4096]{1,0:T(8,128)(2,1)S(1)}, u32[]{:S(2)}, u32[]{:S(2)}) collective-permute-start(bf16[224,4096]{1,0:T(8,128)(2,1)S(1)} %get-tuple-element.10), channel_id=1, source_target_pairs={{0,16},{8,24},{16,0},{24,8},{1,17},{9,25},{17,1},{25,9},{2,18},{10... | collective-permute-start | bytes 5505032 | tf_op jit(solution)/shard_map/ppermute | solution.py:230
  58.2 44.2 %collective-permute-start.1 = (bf16[224,4096]{1,0:T(8,128)(2,1)S(1)}, bf16[224,4096]{1,0:T(8,128)(2,1)}, u32[]{:S(2)}, u32[]{:S(2)}) collective-permute-start(bf16[224,4096]{1,0:T(8,128)(2,1)S(1)} %get-tuple-element.10), channel_id=1, source_target_pairs={{0,8},{8,0},{16,24},{24,16},{1,9},{9,1},{17,25},{25,17},{2,10},{10... | collective-permute-start | bytes 5505032 | tf_op jit(solution)/shard_map/ppermute | solution.py:230
  61.1 60.0 %collective-permute-start.6 = (bf16[112,4096]{1,0:T(8,128)(2,1)S(1)}, bf16[112,4096]{1,0:T(8,128)(2,1)}, u32[]{:S(2)}, u32[]{:S(2)}) collective-permute-start(bf16[112,4096]{1,0:T(8,128)(2,1)S(1)} %slice.134), channel_id=1, source_target_pairs={{0,16},{8,24},{16,0},{24,8},{1,17},{9,25},{17,1},{25,9},{2,18},{10... | collective-permute-start | bytes 2752520 | tf_op jit(solution)/shard_map/ppermute | solution.py:230
  64.0 57.2 %collective-permute-start.7 = (bf16[112,4096]{1,0:T(8,128)(2,1)S(1)}, bf16[112,4096]{1,0:T(8,128)(2,1)}, u32[]{:S(2)}, u32[]{:S(2)}) collective-permute-start(bf16[112,4096]{1,0:T(8,128)(2,1)S(1)} %slice.135), channel_id=1, source_target_pairs={{0,8},{8,0},{16,24},{24,16},{1,9},{9,1},{17,25},{25,17},{2,10},{10... | collective-permute-start | bytes 2752520 | tf_op jit(solution)/shard_map/ppermute | solution.py:230
  100.8 37.3 %collective-permute-start.10 = (bf16[112,4096]{1,0:T(8,128)(2,1)S(1)}, bf16[112,4096]{1,0:T(8,128)(2,1)S(1)}, u32[]{:S(2)}, u32[]{:S(2)}) collective-permute-start(bf16[112,4096]{1,0:T(8,128)(2,1)S(1)} %slice.137), channel_id=1, source_target_pairs={{0,8},{8,0},{16,24},{24,16},{1,9},{9,1},{17,25},{25,17},{2,10},{10... | collective-permute-start | bytes 2752520 | tf_op jit(solution)/shard_map/ppermute | solution.py:230
  103.6 35.5 %collective-permute-start.9 = (bf16[112,4096]{1,0:T(8,128)(2,1)S(1)}, bf16[112,4096]{1,0:T(8,128)(2,1)S(1)}, u32[]{:S(2)}, u32[]{:S(2)}) collective-permute-start(bf16[112,4096]{1,0:T(8,128)(2,1)S(1)} %slice.136), channel_id=1, source_target_pairs={{0,16},{8,24},{16,0},{24,8},{1,17},{9,25},{17,1},{25,9},{2,18},{10... | collective-permute-start | bytes 2752520 | tf_op jit(solution)/shard_map/ppermute | solution.py:230
  131.2 23.7 %copy-start.13 = (s32[1,224,32]{1,2,0:T(8,128)S(1)}, s32[1,224,32]{1,2,0:T(8,128)}, u32[]{:S(2)}) copy-start(s32[1,224,32]{1,2,0:T(8,128)} %param.13) | copy-start | bytes 86020
  154.7 49.4 %copy-start.12 = (s32[1,224,32]{1,2,0:T(8,128)S(1)}, s32[1,224,32]{1,2,0:T(8,128)}, u32[]{:S(2)}) copy-start(s32[1,224,32]{1,2,0:T(8,128)} %param.14) | copy-start | bytes 86020
  198.3 135.5 %all-to-all-start = ((s32[32,1,560]{2,1,0:T(1,128)}), s32[32,1,560]{2,1,0:T(1,128)S(1)}, u32[]{:S(2)}, u32[]{:S(2)}) async-start(s32[32,1,560]{2,1,0:T(1,128)} %all_to_all.12), calls=%async_computation | async-start | bytes 163840 | tf_op jit(solution)/shard_map/all_to_all | solution.py:295
  223.4 23.7 %slice-start = ((s8[25165824]{0:T(1024)(128)(4,1)}), s8[4194304]{0:T(1024)(128)(4,1)S(1)}, s32[]{:S(2)}) async-start(s8[25165824]{0:T(1024)(128)(4,1)} %bitcast.152), calls=%async_computation.4 | async-start | bytes 8388608
  223.4 23.7 %slice-start.1 = ((s8[25165824]{0:T(1024)(128)(4,1)}), s8[4194304]{0:T(1024)(128)(4,1)S(1)}, s32[]{:S(2)}) async-start(s8[25165824]{0:T(1024)(128)(4,1)} %bitcast.152), calls=%async_computation.5 | async-start | bytes 8388608
  231.1 41.1 %collective-permute-start.12 = (bf16[448,2048]{1,0:T(8,128)(2,1)}, bf16[448,2048]{1,0:T(8,128)(2,1)S(1)}, u32[]{:S(2)}, u32[]{:S(2)}) collective-permute-start(bf16[448,2048]{1,0:T(8,128)(2,1)} %fusion.66), channel_id=1, source_target_pairs={{0,16},{8,24},{16,0},{24,8},{1,17},{9,25},{17,1},{25,9},{2,18},{10... | collective-permute-start | bytes 5505032 | tf_op jit(solution)/shard_map/ppermute | solution.py:230
  240.4 43.1 %collective-permute-start.11 = (bf16[448,2048]{1,0:T(8,128)(2,1)}, bf16[448,2048]{1,0:T(8,128)(2,1)S(1)}, u32[]{:S(2)}, u32[]{:S(2)}) collective-permute-start(bf16[448,2048]{1,0:T(8,128)(2,1)} %fusion.60), channel_id=1, source_target_pairs={{0,8},{8,0},{16,24},{24,16},{1,9},{9,1},{17,25},{25,17},{2,10},{10... | collective-permute-start | bytes 5505032 | tf_op jit(solution)/shard_map/ppermute | solution.py:230
  250.2 35.8 %copy-start.6 = (bf16[448,2048]{1,0:T(8,128)(2,1)}, bf16[448,2048]{1,0:T(8,128)(2,1)S(1)}, u32[]{:S(2)}) copy-start(bf16[448,2048]{1,0:T(8,128)(2,1)S(1)} %fusion.63.refs_3_) | copy-start | bytes 5505028
  272.5 28.0 %collective-permute-start.14 = (bf16[224,2048]{1,0:T(8,128)(2,1)S(1)}, bf16[224,2048]{1,0:T(8,128)(2,1)}, u32[]{:S(2)}, u32[]{:S(2)}) collective-permute-start(bf16[224,2048]{1,0:T(8,128)(2,1)S(1)} %add_convert_fusion.2), channel_id=1, source_target_pairs={{0,8},{8,0},{16,24},{24,16},{1,9},{9,1},{17,25},{25,17},{2,10},{10... | collective-permute-start | bytes 2752520 | tf_op jit(solution)/shard_map/ppermute | solution.py:230
  286.0 17.3 %collective-permute-start.13 = (bf16[224,2048]{1,0:T(8,128)(2,1)}, bf16[224,2048]{1,0:T(8,128)(2,1)}, u32[]{:S(2)}, u32[]{:S(2)}) collective-permute-start(bf16[224,2048]{1,0:T(8,128)(2,1)} %add_convert_fusion.3), channel_id=1, source_target_pairs={{0,16},{8,24},{16,0},{24,8},{1,17},{9,25},{17,1},{25,9},{2,18},{10... | collective-permute-start | bytes 2752520 | tf_op jit(solution)/shard_map/ppermute | solution.py:230
  333.8 154.4 %all-to-all-start.1 = ((bf16[32,560,128]{2,1,0:T(8,128)(2,1)}), bf16[32,560,128]{2,1,0:T(8,128)(2,1)}, u32[]{:S(2)}, u32[]{:S(2)}) async-start(bf16[32,560,128]{2,1,0:T(8,128)(2,1)} %bitcast.154), calls=%async_computation.1 | async-start | bytes 9175040 | tf_op jit(solution)/shard_map/all_to_all | solution.py:449
  337.4 89.9 %copy-start.17 = (bf16[896,1536]{1,0:T(8,128)(2,1)S(1)}, bf16[896,1536]{1,0:T(8,128)(2,1)}, u32[]{:S(2)}) copy-start(bf16[896,1536]{1,0:T(8,128)(2,1)} %get-tuple-element.8) | copy-start | bytes 8257540
  337.4 86.5 %collective-permute-start.17 = (bf16[448,2048]{1,0:T(8,128)(2,1)}, bf16[448,2048]{1,0:T(8,128)(2,1)S(1)}, u32[]{:S(2)}, u32[]{:S(2)}) collective-permute-start(bf16[448,2048]{1,0:T(8,128)(2,1)} %fusion.72), channel_id=1, source_target_pairs={{0,16},{8,24},{16,0},{24,8},{1,17},{9,25},{17,1},{25,9},{2,18},{10... | collective-permute-start | bytes 5505032 | tf_op jit(solution)/shard_map/ppermute | solution.py:230
  339.1 88.2 %collective-permute-start.15 = (bf16[448,2048]{1,0:T(8,128)(2,1)}, bf16[448,2048]{1,0:T(8,128)(2,1)S(1)}, u32[]{:S(2)}, u32[]{:S(2)}) collective-permute-start(bf16[448,2048]{1,0:T(8,128)(2,1)} %fusion.69), channel_id=1, source_target_pairs={{0,8},{8,0},{16,24},{24,16},{1,9},{9,1},{17,25},{25,17},{2,10},{10... | collective-permute-start | bytes 5505032 | tf_op jit(solution)/shard_map/ppermute | solution.py:230
  346.8 85.6 %copy-start.5 = (bf16[448,2048]{1,0:T(8,128)(2,1)}, bf16[448,2048]{1,0:T(8,128)(2,1)S(1)}, u32[]{:S(2)}) copy-start(bf16[448,2048]{1,0:T(8,128)(2,1)S(1)} %fusion.75.refs_3_) | copy-start | bytes 5505028
  424.2 28.3 %collective-permute-start.18 = (bf16[224,2048]{1,0:T(8,128)(2,1)S(1)}, bf16[224,2048]{1,0:T(8,128)(2,1)}, u32[]{:S(2)}, u32[]{:S(2)}) collective-permute-start(bf16[224,2048]{1,0:T(8,128)(2,1)S(1)} %add_convert_fusion), channel_id=1, source_target_pairs={{0,8},{8,0},{16,24},{24,16},{1,9},{9,1},{17,25},{25,17},{2,10},{10... | collective-permute-start | bytes 2752520 | tf_op jit(solution)/shard_map/ppermute | solution.py:230
  432.4 25.3 %collective-permute-start.16 = (bf16[224,2048]{1,0:T(8,128)(2,1)S(1)}, bf16[224,2048]{1,0:T(8,128)(2,1)}, u32[]{:S(2)}, u32[]{:S(2)}) collective-permute-start(bf16[224,2048]{1,0:T(8,128)(2,1)S(1)} %add_convert_fusion.1), channel_id=1, source_target_pairs={{0,16},{8,24},{16,0},{24,8},{1,17},{9,25},{17,1},{25,9},{2,18},{10... | collective-permute-start | bytes 2752520 | tf_op jit(solution)/shard_map/ppermute | solution.py:230
  488.2 108.6 %all-to-all-start.2 = ((bf16[32,560,128]{2,1,0:T(8,128)(2,1)}), bf16[32,560,128]{2,1,0:T(8,128)(2,1)}, u32[]{:S(2)}, u32[]{:S(2)}) async-start(bf16[32,560,128]{2,1,0:T(8,128)(2,1)} %bitcast.155), calls=%async_computation.2 | async-start | bytes 9175040 | tf_op jit(solution)/shard_map/all_to_all | solution.py:449
  596.8 25.4 %copy-start.1 = (f32[8,4]{0,1:T(4,128)S(1)}, f32[8,4]{0,1:T(4,128)}, u32[]{:S(2)}) copy-start(f32[8,4]{0,1:T(4,128)} %param.15) | copy-start | bytes 388
  (15 other events, 140.9 us)
Sparse Core Ops, SparseCore 0:
  154.8 62.5 all-reduce.1
